TPU v7x, 32 devices: a whole 2x2x4 slice. The times are simulated.
32 devices in a mesh: gx: 8 (over z, x), gy: 2 (over y), pa: 2 (over core).
Axes of the slice: x: 2, y: 2, z: 4, core: 2. Of those that a mesh axis runs over, the one named last changes fastest.
Arguments:
- leaf_maps: bfloat16 [8, 2, 2, 1024, 1024], P('gx', 'gy', None, 'pa'), may hold values from -0.125 to 0.125
- face_index: int32 [8, 2, 1024], P('gx', 'gy'), may hold values from 0 to 1023, each once within a row
- order_x: int32 [4, 2], replicated, may hold values from 0 to 1
- order_y: int32 [4, 1], replicated, may hold values from 0 to 1
- traces: float32 [8, 2, 2, 1024], P('gx', 'gy'), may hold values from -6 to 6
Outputs:
- merged_map: bfloat16 [8, 2, 2, 2, 128, 1024], P('gx', 'gy', 'pa')
- outgoing: float32 [8, 2, 2, 2, 128], P('gx', 'gy', 'pa')
Inputs may be any that keep to these rules, and one draw needn't show every extreme that they name: `face_index`: each row is a permutation of 0 to 1023.
All inputs are finite; a program needn't handle non-finite values.
Results may differ from a plain program's by a relative error of at most 0.0058.
Values may be sent and summed in bfloat16 or wider, within the bound.
A program may use at most 64 MiB of HBM per device.

v0:
```python
import jax
import jax.numpy as jnp
from jax import lax
from jax.sharding import PartitionSpec as P


def from_partner(value, axis, apart):
    mask = 2**apart
    pairs = [(source, source ^ mask) for source in range(lax.axis_size(axis))]
    return lax.ppermute(value, axis, pairs)


def complex_rows(left_block, right_block):
    real_part = jnp.dot(
        left_block[0], right_block[0], preferred_element_type=jnp.float32
    ) - jnp.dot(left_block[1], right_block[1], preferred_element_type=jnp.float32)
    imag_part = jnp.dot(
        left_block[0], right_block[1], preferred_element_type=jnp.float32
    ) + jnp.dot(left_block[1], right_block[0], preferred_element_type=jnp.float32)
    return (real_part, imag_part)


def folder(left_rows, segment):
    real_part, imag_part = complex_rows(left_rows, segment)
    return (real_part, imag_part)


def per_device(leaf_maps, face_index, order_x, order_y, traces):
    own_panel = jnp.take(leaf_maps[0, 0], face_index[0, 0], axis=2)
    panel_rows = own_panel.shape[1]
    width = own_panel.shape[2]
    half_rows = panel_rows // 2
    quarter = panel_rows // 4
    half_index = lax.axis_index("gx") % 2
    vert_index = lax.axis_index("gy") % 2
    pair_index = lax.axis_index("gx") // 2
    column_index = lax.axis_index("gy")
    first_bit = order_x[pair_index, column_index]
    sibling = from_partner(own_panel, "gx", 0)
    right_panel = jnp.where(half_index == first_bit, own_panel, sibling)
    left_panel = jnp.where(half_index == first_bit, sibling, own_panel)
    left_rows = lax.dynamic_slice_in_dim(left_panel, half_index * half_rows, half_rows, 1)
    blocks = lax.all_to_all(left_rows, "pa", split_axis=2, concat_axis=1, tiled=True)
    real_part, imag_part = complex_rows(blocks, right_panel)
    summed = lax.psum_scatter(
        jnp.concatenate([real_part, imag_part], axis=1), "pa", scatter_dimension=0, tiled=True
    )
    real_one = summed[:, :width]
    imag_one = summed[:, width:]
    merged_one = jnp.stack([real_one, imag_one]).astype(jnp.bfloat16)
    second_bit = order_y[pair_index, column_index // 2]
    other_box = from_partner(merged_one, "gy", 0)
    right_two = jnp.where(vert_index == second_bit, merged_one, other_box)
    left_two = jnp.where(vert_index == second_bit, other_box, merged_one)
    left_rows_two = lax.dynamic_slice_in_dim(left_two, vert_index * quarter, quarter, 1)
    other_half = from_partner(right_two, "gx", 0)
    first_part = jnp.where(half_index == 0, right_two, other_half)
    second_part = jnp.where(half_index == 0, other_half, right_two)
    full_panel = jnp.concatenate([first_part, second_part], axis=1)
    real_two, imag_two = folder(left_rows_two, lax.all_gather(full_panel, "pa", axis=1, tiled=True))
    merged_two = jnp.stack([real_two, imag_two]).astype(jnp.bfloat16)
    trace_sum = traces[0, 0] + from_partner(traces[0, 0], "gx", 0)
    trace_sum = trace_sum + from_partner(trace_sum, "gy", 0)
    wide = merged_two.astype(jnp.float32)
    highest = lax.Precision.HIGHEST
    real_out = jnp.dot(wide[0], trace_sum[0], precision=highest) - jnp.dot(
        wide[1], trace_sum[1], precision=highest
    )
    imag_out = jnp.dot(wide[0], trace_sum[1], precision=highest) + jnp.dot(
        wide[1], trace_sum[0], precision=highest
    )
    outgoing = jnp.stack([real_out, imag_out]).reshape(1, 1, 1, 2, quarter)
    return (merged_two.reshape(1, 1, 1, 2, quarter, width), outgoing)


def solution(mesh):
    placed = (
        P("gx", "gy", None, "pa", None),
        P("gx", "gy", None),
        P(),
        P(),
        P("gx", "gy", None, None),
    )
    return jax.shard_map(
        per_device,
        mesh=mesh,
        in_specs=placed,
        out_specs=(P("gx", "gy", "pa", None, None, None), P("gx", "gy", "pa", None, None)),
        check_vma=False,
    )
```

profile of v0, /device:TPU:0, one launch (start us, length us, event | category | flops | bytes accessed | tf_op | source)
XLA Modules:
  0.0 207.1 jit_solution(6228542808558593444)
XLA Ops:
  7.2 0.0 copy-start
  7.2 0.0 copy-start.3
  7.2 0.0 reduce-scatter.2.cloned.1.call-start
  7.2 6.2 %copy.9 = bf16[1,1,2,512,1024]{3,2,4,1,0:T(2,128)(2,1)} copy(bf16[1,1,2,512,1024]{4,3,2,1,0:T(8,128)(2,1)} %param.5) | data formatting | bytes 4194304 | tf_op args[0]
  13.4 0.0 copy-done.3
  13.4 7.5 %gather_fusion = bf16[1024,2,512]{2,1,0:T(2,128)(2,1)S(1)} fusion(bf16[2,512,1024]{1,0,2:T(2,128)(2,1)} %bitcast.99, s32[1024]{0:T(1024)S(1)} %broadcast_clamp_fusion), kind=kCustom, calls=%fused_computation | custom fusion | bytes 4198400 | tf_op jit(solution)/shard_map/jit(_take)/gather | solution.py:29
  20.9 0.0 copy-start.5
  20.9 4.6 %fusion = bf16[2,512,1024]{1,0,2:T(2,128)(2,1)} fusion(bf16[1024,2,512]{2,1,0:T(2,128)(2,1)S(1)} %gather_fusion, pred[1024]{0:T(1024)(128)(4,1)S(1)} %compare_and_fusion), kind=kLoop, calls=%fused_computation.7 | loop fusion | flops 1048576 | bytes 4195328 | tf_op jit(solution)/shard_map/jit(_take)/select_n | solution.py:29
  25.5 3.0 %collective-permute-start = (bf16[2,512,1024]{1,0,2:T(2,128)(2,1)}, bf16[2,512,1024]{1,0,2:T(2,128)(2,1)}, u32[]{:S(2)}, u32[]{:S(2)}) collective-permute-start(bf16[2,512,1024]{1,0,2:T(2,128)(2,1)} %fusion), channel_id=1, source_target_pairs={{0,4},{4,0},{8,12},{12,8},{16,20},{20,16},{24,28},{28,24},{1,5},{5... | collective-permute-start | bytes 6291464 | tf_op jit(solution)/shard_map/ppermute | solution.py:10
  28.5 0.0 copy-done.5
  28.5 0.6 dynamic_slice.14
  29.7 44.7 %collective-permute-done = bf16[2,512,1024]{1,0,2:T(2,128)(2,1)} collective-permute-done((bf16[2,512,1024]{1,0,2:T(2,128)(2,1)}, bf16[2,512,1024]{1,0,2:T(2,128)(2,1)}, u32[]{:S(2)}, u32[]{:S(2)}) %collective-permute-start) | collective-permute-done | bytes 2097184 | tf_op jit(solution)/shard_map/ppermute | solution.py:10
  74.4 2.6 %broadcast_select_fusion.2 = bf16[2,256,1024]{1,0,2:T(2,128)(2,1)S(1)} fusion(pred[]{:T(512)S(6)} %eq.16, bf16[2,512,1024]{1,0,2:T(2,128)(2,1)} %fusion, s32[]{:T(128)S(6)} %select_n.95, bf16[2,512,1024]{1,0,2:T(2,128)(2,1)} %collective-permute-done), kind=kLoop, calls=%fused_computation.8 | loop fusion | flops 524288 | bytes 3145733 | tf_op jit(solution)/shard_map/jit(_where)/select_n | solution.py:41
  77.0 5.4 %all_to_all.15 = bf16[2,256,1024]{1,0,2:T(2,128)(2,1)} all-to-all(bf16[2,256,1024]{1,0,2:T(2,128)(2,1)S(1)} %broadcast_select_fusion.2), channel_id=1, replica_groups=mesh['gx'=8,'gy'=2,'pa'=2] {'pa'}, dimensions={2} | all-to-all | bytes 2097152 | tf_op jit(solution)/shard_map/all_to_all | solution.py:43
  82.4 2.4 %copy.10 = bf16[2,256,2,512]{3,1,2,0:T(8,128)(2,1)S(1)} copy(bf16[2,256,2,512]{1,0,3,2:T(2,128)(2,1)} %bitcast.105) | data formatting | bytes 2097152 | tf_op jit(solution)/shard_map/all_to_all | solution.py:43
  84.9 1.0 fusion.22
  85.9 4.9 %broadcast_select_fusion.1 = bf16[2,512,1024]{1,0,2:T(2,128)(2,1)S(1)} fusion(bf16[2,512,1024]{1,0,2:T(2,128)(2,1)} %collective-permute-done, pred[]{:T(512)S(6)} %eq.16, bf16[1024,2,512]{2,1,0:T(2,128)(2,1)S(1)} %gather_fusion, pred[1024]{0:T(1024)(128)(4,1)S(1)} %compare_and_fusion), kind=kLoop, calls=%fused_computation.3 | loop fusion | flops 2097152 | bytes 6292481 | tf_op jit(solution)/shard_map/jit(_where)/select_n | solution.py:40
  90.8 3.8 %fusion.21 = (bf16[1,512,1024]{1,0,2:T(2,128)(2,1)}, bf16[1,512,1024]{1,0,2:T(2,128)(2,1)S(1)}) fusion(bf16[2,512,1024]{1,0,2:T(2,128)(2,1)S(1)} %broadcast_select_fusion.1), kind=kLoop, calls=%fused_computation.55 | loop fusion | bytes 4194304 | tf_op jit(solution)/shard_map/slice | solution.py:16
  94.7 2.6 %copy.11 = bf16[1,512,1024]{2,1,0:T(8,128)(2,1)S(1)} copy(bf16[1,512,1024]{1,0,2:T(2,128)(2,1)S(1)} %get-tuple-element.5) | data formatting | bytes 2097152 | tf_op jit(solution)/shard_map/slice | solution.py:15
  97.3 0.0 copy-start.1
  97.3 4.6 %copy.12 = bf16[1,512,1024]{2,1,0:T(8,128)(2,1)S(1)} copy(bf16[1,512,1024]{1,0,2:T(2,128)(2,1)} %get-tuple-element.4) | data formatting | bytes 2097152 | tf_op jit(solution)/shard_map/slice | solution.py:16
  101.9 0.0 copy-done.1
  101.9 0.7 fusion.16
  102.6 0.0 copy-start.2
  102.7 0.7 fusion.14
  103.4 0.3 copy-done.2
  103.7 0.7 convolution_add_fusion
  104.4 0.7 convolution_subtract_fusion
  105.1 2.5 %pad_maximum_fusion = f32[512,2048]{1,0:T(8,128)} fusion(f32[512,1024]{1,0:T(8,128)S(1)} %convolution_add_fusion, f32[512,1024]{1,0:T(8,128)S(1)} %convolution_subtract_fusion), kind=kLoop, calls=%fused_computation.1 | loop fusion | flops 1048576 | bytes 8388608 | tf_op jit(solution)/shard_map/concatenate | solution.py:46
  107.6 0.0 reduce-scatter.2.cloned.1.call-update
  107.6 0.0 all-gather.2.cloned.1.call-start
  107.7 14.7 %reduce-scatter.2.cloned.1.call-done = f32[256,2048]{1,0:T(8,128)} async-done(((f32[512,2048]{1,0:T(8,128)}), f32[256,2048]{1,0:T(8,128)}) %reduce-scatter.2.cloned.1.call-update) | async-done | bytes 2097168 | tf_op jit(solution)/shard_map/reduce_scatter | solution.py:45
  122.3 1.7 convert.20
  124.1 0.1 slice_bitcast_fusion.15
  124.2 0.1 pad_maximum_fusion.2
  124.3 1.9 collective-permute-start.1
  126.2 0.0 copy-done
  126.2 0.6 constant_dynamic-slice_fusion
  127.4 22.3 %collective-permute-done.1 = bf16[2,256,1024]{2,1,0:T(8,128)(2,1)S(1)} collective-permute-done((bf16[2,256,1024]{2,1,0:T(8,128)(2,1)S(1)}, bf16[2,256,1024]{2,1,0:T(8,128)(2,1)S(1)}, u32[]{:S(2)}, u32[]{:S(2)}) %collective-permute-start.1) | collective-permute-done | bytes 1048608 | tf_op jit(solution)/shard_map/ppermute | solution.py:10
  149.7 0.1 broadcast_select_fusion.5
  149.9 1.8 collective-permute-start.2
  151.6 23.0 %collective-permute-done.2 = bf16[2,256,1024]{2,1,0:T(8,128)(2,1)} collective-permute-done((bf16[2,256,1024]{2,1,0:T(8,128)(2,1)S(1)}, bf16[2,256,1024]{2,1,0:T(8,128)(2,1)}, u32[]{:S(2)}, u32[]{:S(2)}) %collective-permute-start.2) | collective-permute-done | bytes 1048608 | tf_op jit(solution)/shard_map/ppermute | solution.py:10
  174.6 1.5 broadcast_select_fusion.4
  176.1 1.5 pad_maximum_fusion.1
  177.6 0.0 all-gather.2.cloned.1.call-update
  177.6 0.7 copy-done.4
  178.3 1.5 collective-permute-start.3
  179.8 2.1 %collective-permute-done.3 = f32[2,1024]{1,0:T(2,128)S(1)} collective-permute-done((f32[2,1024]{1,0:T(2,128)S(1)}, f32[2,1024]{1,0:T(2,128)S(1)}, u32[]{:S(2)}, u32[]{:S(2)}) %collective-permute-start.3) | collective-permute-done | bytes 8224 | tf_op jit(solution)/shard_map/ppermute | solution.py:10
  182.0 1.5 collective-permute-start.4
  183.5 2.1 %collective-permute-done.4 = f32[2,1024]{1,0:T(2,128)S(1)} collective-permute-done((f32[2,1024]{1,0:T(2,128)S(1)}, f32[2,1024]{1,0:T(2,128)S(1)}, u32[]{:S(2)}, u32[]{:S(2)}) %collective-permute-start.4) | collective-permute-done | bytes 8224 | tf_op jit(solution)/shard_map/ppermute | solution.py:10
  185.6 0.2 fusion.20
  185.8 6.5 %all-gather.2.cloned.1.call-done = bf16[2,1024,1024]{2,1,0:T(8,128)(2,1)} async-done(((bf16[2,512,1024]{2,1,0:T(8,128)(2,1)}), bf16[2,1024,1024]{2,1,0:T(8,128)(2,1)}) %all-gather.2.cloned.1.call-update) | async-done | bytes 4194320 | tf_op jit(solution)/shard_map/all_gather | solution.py:60
  192.4 0.0 copy-start.6
  192.4 2.2 %fusion.1 = f32[128,1024]{1,0:T(8,128)S(1)} fusion(bf16[2,1024,1024]{2,1,0:T(8,128)(2,1)} %all-gather.2.cloned.1.call-done, bf16[2,128,1024]{2,1,0:T(8,128)(2,1)S(1)} %fusion.20), kind=kOutput, calls=%fused_computation.9 | convolution fusion | flops 268435456 | bytes 2883584 | tf_op jit(solution)/shard_map/dot_general | solution.py:19
  194.6 2.1 fusion.8
  196.6 0.3 convolution_bitcast_fusion
  196.9 0.3 convolution_bitcast_fusion.2
  197.3 0.0 copy-done.6
  197.3 0.5 fusion.4
  197.8 0.5 fusion.7
  198.2 0.2 fusion.10
  198.4 0.4 fusion.12
  198.8 0.9 pad_maximum_fusion.3
  199.7 0.6 maximum_bitcast_fusion
  (6 shorter events, 0.0 us)
Async XLA Ops:
  7.2 119.0 %copy-start = (s32[4,1]{0,1:T(1,128)S(1)}, s32[4,1]{0,1:T(1,128)}, u32[]{:S(2)}) copy-start(s32[4,1]{0,1:T(1,128)} %param.8) | copy-start | bytes 52
  7.2 6.2 %copy-start.3 = (s32[1,1,1024]{2,1,0:T(1,128)S(1)}, s32[1,1,1024]{2,1,0:T(1,128)}, u32[]{:S(2)}) copy-start(s32[1,1,1024]{2,1,0:T(1,128)} %param.6) | copy-start | bytes 12292
  7.2 115.2 %reduce-scatter.2.cloned.1.call-start = ((), (), s32[]{:S(2)}) async-start(), calls=%async_computation.2 | async-start | bytes 6291456 | tf_op jit(solution)/shard_map/reduce_scatter | solution.py:45
  20.9 7.6 %copy-start.5 = (s32[4,2]{0,1:T(2,128)S(1)}, s32[4,2]{0,1:T(2,128)}, u32[]{:S(2)}) copy-start(s32[4,2]{0,1:T(2,128)} %param.7) | copy-start | bytes 100
  25.5 48.9 %collective-permute-start = (bf16[2,512,1024]{1,0,2:T(2,128)(2,1)}, bf16[2,512,1024]{1,0,2:T(2,128)(2,1)}, u32[]{:S(2)}, u32[]{:S(2)}) collective-permute-start(bf16[2,512,1024]{1,0,2:T(2,128)(2,1)} %fusion), channel_id=1, source_target_pairs={{0,4},{4,0},{8,12},{12,8},{16,20},{20,16},{24,28},{28,24},{1,5},{5... | collective-permute-start | bytes 6291464 | tf_op jit(solution)/shard_map/ppermute | solution.py:10
  97.3 4.6 %copy-start.1 = (bf16[1,2,256,512]{3,2,1,0:T(8,128)(2,1)S(1)}, bf16[1,2,256,512]{3,2,1,0:T(8,128)(2,1)}, u32[]{:S(2)}) copy-start(bf16[1,2,256,512]{3,2,1,0:T(8,128)(2,1)} %get-tuple-element.9) | copy-start | bytes 1572868
  102.6 1.0 copy-start.2
  107.6 84.8 %all-gather.2.cloned.1.call-start = ((), (), s32[]{:S(2)}) async-start(), calls=%async_computation.3 | async-start | bytes 6291456 | tf_op jit(solution)/shard_map/all_gather | solution.py:60
  124.3 25.5 %collective-permute-start.1 = (bf16[2,256,1024]{2,1,0:T(8,128)(2,1)S(1)}, bf16[2,256,1024]{2,1,0:T(8,128)(2,1)S(1)}, u32[]{:S(2)}, u32[]{:S(2)}) collective-permute-start(bf16[2,256,1024]{2,1,0:T(8,128)(2,1)S(1)} %pad_maximum_fusion.2), channel_id=1, source_target_pairs={{0,2},{2,0},{1,3},{3,1},{4,6},{6,4},{5,7},{7,5},{8,10},{10,8},{9,1... | collective-permute-start | bytes 3145736 | tf_op jit(solution)/shard_map/ppermute | solution.py:10
  149.9 24.7 %collective-permute-start.2 = (bf16[2,256,1024]{2,1,0:T(8,128)(2,1)S(1)}, bf16[2,256,1024]{2,1,0:T(8,128)(2,1)}, u32[]{:S(2)}, u32[]{:S(2)}) collective-permute-start(bf16[2,256,1024]{2,1,0:T(8,128)(2,1)S(1)} %broadcast_select_fusion.5), channel_id=1, source_target_pairs={{0,4},{4,0},{8,12},{12,8},{16,20},{20,16},{24,28},{28,24},{1,5},{5... | collective-permute-start | bytes 3145736 | tf_op jit(solution)/shard_map/ppermute | solution.py:10
  177.6 0.7 copy-start.4
  178.3 3.7 %collective-permute-start.3 = (f32[2,1024]{1,0:T(2,128)S(1)}, f32[2,1024]{1,0:T(2,128)S(1)}, u32[]{:S(2)}, u32[]{:S(2)}) collective-permute-start(f32[2,1024]{1,0:T(2,128)S(1)} %bitcast.110), channel_id=1, source_target_pairs={{0,4},{4,0},{8,12},{12,8},{16,20},{20,16},{24,28},{28,24},{1,5},{5... | collective-permute-start | bytes 24584 | tf_op jit(solution)/shard_map/ppermute | solution.py:10
  182.0 3.7 %collective-permute-start.4 = (f32[2,1024]{1,0:T(2,128)S(1)}, f32[2,1024]{1,0:T(2,128)S(1)}, u32[]{:S(2)}, u32[]{:S(2)}) collective-permute-start(f32[2,1024]{1,0:T(2,128)S(1)} %bitcast_add_fusion), channel_id=1, source_target_pairs={{0,2},{2,0},{1,3},{3,1},{4,6},{6,4},{5,7},{7,5},{8,10},{10,8},{9,1... | collective-permute-start | bytes 24584 | tf_op jit(solution)/shard_map/ppermute | solution.py:10
  192.4 4.9 %copy-start.6 = (bf16[2,1024,1024]{2,1,0:T(8,128)(2,1)S(1)}, bf16[2,1024,1024]{2,1,0:T(8,128)(2,1)}, u32[]{:S(2)}) copy-start(bf16[2,1024,1024]{2,1,0:T(8,128)(2,1)} %all-gather.2.cloned.1.call-done) | copy-start | bytes 12582916
Sparse Core Ops, SparseCore 0:
  107.7 14.5 reduce-scatter.1
  177.8 14.5 all-gather.1
where the time goes:
time: 208 us; the launch traced here: 207 us
  waiting for transfers between devices  115 us (55%)
  local copies, waits for them, and re-layouts  30.4 us (15%)
  other arithmetic  21.2 us (10%)
  between operations  15.6 us (8%)
  starting transfers between devices  9.77 us (5%)
  matrix products  9.28 us (4%)
  blocking collectives  5.37 us (3%)
    ppermute x5, waiting for transfers between devices, from_partner(): return lax.ppermute(value, axis, pairs)  94.2 us
    reduce_scatter x1, waiting for transfers between devices, per_device(): lax.psum_scatter(jnp.concatenate([real_part, imag_part], axis=1), 'pa', s...  14.7 us
    ppermute x5, starting transfers between devices, from_partner(): return lax.ppermute(value, axis, pairs)  9.69 us
    slice x2, local copies, waits for them, and re-layouts, complex_rows(): right_block[1]  8.47 us
    gather x1, local copies, waits for them, and re-layouts, per_device(): own_panel = jnp.take(leaf_maps[0, 0], face_index[0, 0], axis=2)  7.46 us
    unnamed x15, local copies, waits for them, and re-layouts  7.18 us
    all_gather x1, waiting for transfers between devices, per_device(): lax.all_gather(full_panel, 'pa', axis=1, tiled=True)  6.54 us
    all_to_all x1, blocking collectives, per_device(): lax.all_to_all(left_rows, 'pa', split_axis=2, concat_axis=1, tiled=True)  5.37 us
  transfers between devices with their start and end apart: 7, of which 7 were waited for; matrix products, arithmetic and copies ran while one was open for 1% of the time, Pallas kernels for 0%

commit v1 on v0

--- a/solution.py
+++ b/solution.py
@@ -40,7 +40,9 @@
     right_panel = jnp.where(half_index == first_bit, own_panel, sibling)
     left_panel = jnp.where(half_index == first_bit, sibling, own_panel)
     left_rows = lax.dynamic_slice_in_dim(left_panel, half_index * half_rows, half_rows, 1)
-    blocks = lax.all_to_all(left_rows, "pa", split_axis=2, concat_axis=1, tiled=True)
+    blocks = jnp.concatenate(
+        lax.all_to_all(jnp.stack(jnp.split(left_rows, lax.axis_size("pa"), 2)), "pa", 0, 0), axis=1
+    )
     real_part, imag_part = complex_rows(blocks, right_panel)
     summed = lax.psum_scatter(
         jnp.concatenate([real_part, imag_part], axis=1), "pa", scatter_dimension=0, tiled=True

time: 208 us -> 212 us (1.019)
  local copies, waits for them, and re-layouts: 30.4 us -> 34.3 us
    slice x1 -> x2, local copies, waits for them, and re-layouts: 1.04 us -> 4.67 us  [complex_rows(): left_block[0]]
    all_to_all x1 -> x0, local copies, waits for them, and re-layouts: 2.45 us -> none  [per_device(): lax.all_to_all(left_rows, 'pa', split_axis=2, concat_axis=1, tiled=True)]
    slice x0 -> x1, local copies, waits for them, and re-layouts: none -> 2.28 us  [complex_rows(): left_block[1]]
    unnamed x15 -> x13, local copies, waits for them, and re-layouts: 7.18 us -> 6.86 us
where the time goes in v1:
time: 212 us
  waiting for transfers between devices  115 us (54%)
  local copies, waits for them, and re-layouts  34.3 us (16%)
  other arithmetic  22.7 us (11%)
  between operations  15.6 us (7%)
  starting transfers between devices  9.95 us (5%)
  matrix products  9.29 us (4%)
  blocking collectives  4.58 us (2%)
    ppermute x5, waiting for transfers between devices, from_partner(): return lax.ppermute(value, axis, pairs)  94.2 us
    reduce_scatter x1, waiting for transfers between devices, per_device(): lax.psum_scatter(jnp.concatenate([real_part, imag_part], axis=1), 'pa', s...  14.5 us
    ppermute x5, starting transfers between devices, from_partner(): return lax.ppermute(value, axis, pairs)  9.69 us
    slice x2, local copies, waits for them, and re-layouts, complex_rows(): right_block[1]  8.41 us
    gather x1, local copies, waits for them, and re-layouts, per_device(): own_panel = jnp.take(leaf_maps[0, 0], face_index[0, 0], axis=2)  7.46 us
    unnamed x13, local copies, waits for them, and re-layouts  6.86 us
    all_gather x1, waiting for transfers between devices, per_device(): lax.all_gather(full_panel, 'pa', axis=1, tiled=True)  6.54 us
    select_n x1, other arithmetic, per_device(): right_panel = jnp.where(half_index == first_bit, own_panel, sibling)  4.9 us
  transfers between devices with their start and end apart: 7, of which 7 were waited for; matrix products, arithmetic and copies ran while one was open for 1% of the time, Pallas kernels for 0%

profile of v1, /device:TPU:0, one launch (start us, length us, event | category | flops | bytes accessed | tf_op | source)
XLA Modules:
  0.0 211.6 jit_solution(275536771545331185)
XLA Ops:
  7.2 0.0 copy-start
  7.2 0.0 copy-start.2
  7.2 0.0 reduce-scatter.2.cloned.1.call-start
  7.2 6.2 %copy.8 = bf16[1,1,2,512,1024]{3,2,4,1,0:T(2,128)(2,1)} copy(bf16[1,1,2,512,1024]{4,3,2,1,0:T(8,128)(2,1)} %param.5) | data formatting | bytes 4194304 | tf_op args[0]
  13.4 0.0 copy-done.2
  13.4 7.5 %gather_fusion = bf16[1024,2,512]{2,1,0:T(2,128)(2,1)S(1)} fusion(bf16[2,512,1024]{1,0,2:T(2,128)(2,1)} %bitcast.103, s32[1024]{0:T(1024)S(1)} %broadcast_clamp_fusion), kind=kCustom, calls=%fused_computation | custom fusion | bytes 4198400 | tf_op jit(solution)/shard_map/jit(_take)/gather | solution.py:29
  20.9 0.0 copy-start.4
  20.9 4.6 %fusion = bf16[2,512,1024]{1,0,2:T(2,128)(2,1)} fusion(bf16[1024,2,512]{2,1,0:T(2,128)(2,1)S(1)} %gather_fusion, pred[1024]{0:T(1024)(128)(4,1)S(1)} %compare_and_fusion), kind=kLoop, calls=%fused_computation.7 | loop fusion | flops 1048576 | bytes 4195328 | tf_op jit(solution)/shard_map/jit(_take)/select_n | solution.py:29
  25.5 3.0 %collective-permute-start = (bf16[2,512,1024]{1,0,2:T(2,128)(2,1)}, bf16[2,512,1024]{1,0,2:T(2,128)(2,1)}, u32[]{:S(2)}, u32[]{:S(2)}) collective-permute-start(bf16[2,512,1024]{1,0,2:T(2,128)(2,1)} %fusion), channel_id=1, source_target_pairs={{0,4},{4,0},{8,12},{12,8},{16,20},{20,16},{24,28},{28,24},{1,5},{5... | collective-permute-start | bytes 6291464 | tf_op jit(solution)/shard_map/ppermute | solution.py:10
  28.5 0.0 copy-done.4
  28.5 0.6 dynamic_slice.14
  29.7 44.7 %collective-permute-done = bf16[2,512,1024]{1,0,2:T(2,128)(2,1)} collective-permute-done((bf16[2,512,1024]{1,0,2:T(2,128)(2,1)}, bf16[2,512,1024]{1,0,2:T(2,128)(2,1)}, u32[]{:S(2)}, u32[]{:S(2)}) %collective-permute-start) | collective-permute-done | bytes 2097184 | tf_op jit(solution)/shard_map/ppermute | solution.py:10
  74.4 2.6 %broadcast_select_fusion.2 = bf16[2,256,1024]{1,0,2:T(2,128)(2,1)S(1)} fusion(pred[]{:T(512)S(6)} %eq.16, bf16[2,512,1024]{1,0,2:T(2,128)(2,1)} %fusion, s32[]{:T(128)S(6)} %select_n.95, bf16[2,512,1024]{1,0,2:T(2,128)(2,1)} %collective-permute-done), kind=kLoop, calls=%fused_computation.8 | loop fusion | flops 524288 | bytes 3145733 | tf_op jit(solution)/shard_map/jit(_where)/select_n | solution.py:41
  77.0 0.7 slice_bitcast_fusion.17
  77.8 1.5 pad_maximum_fusion.3
  79.3 4.6 %all_to_all.5 = bf16[2,2,256,512]{2,1,3,0:T(2,128)(2,1)S(1)} all-to-all(bf16[2,2,256,512]{2,1,3,0:T(2,128)(2,1)S(1)} %pad_maximum_fusion.3), channel_id=1, replica_groups=mesh['gx'=8,'gy'=2,'pa'=2] {'pa'}, dimensions={0} | all-to-all | bytes 2097152 | tf_op jit(solution)/shard_map/all_to_all | solution.py:44
  83.8 2.3 %fusion.22 = (bf16[1,2,256,512]{2,0,3,1:T(2,128)(2,1)}, bf16[1,2,256,512]{2,0,3,1:T(2,128)(2,1)S(1)}) fusion(bf16[2,2,256,512]{2,0,3,1:T(2,128)(2,1)S(1)} %bitcast.102), kind=kLoop, calls=%fused_computation.59 | loop fusion | bytes 2097152 | tf_op jit(solution)/shard_map/slice | solution.py:15
  86.1 2.3 %copy.11 = bf16[1,2,256,512]{3,2,1,0:T(8,128)(2,1)} copy(bf16[1,2,256,512]{2,0,3,1:T(2,128)(2,1)S(1)} %get-tuple-element.9) | data formatting | bytes 1048576 | tf_op jit(solution)/shard_map/slice | solution.py:16
  88.4 4.9 %broadcast_select_fusion.1 = bf16[2,512,1024]{1,0,2:T(2,128)(2,1)S(1)} fusion(bf16[2,512,1024]{1,0,2:T(2,128)(2,1)} %collective-permute-done, pred[]{:T(512)S(6)} %eq.16, bf16[1024,2,512]{2,1,0:T(2,128)(2,1)S(1)} %gather_fusion, pred[1024]{0:T(1024)(128)(4,1)S(1)} %compare_and_fusion), kind=kLoop, calls=%fused_computation.3 | loop fusion | flops 2097152 | bytes 6292481 | tf_op jit(solution)/shard_map/jit(_where)/select_n | solution.py:40
  93.3 3.8 %fusion.21 = (bf16[1,512,1024]{1,0,2:T(2,128)(2,1)}, bf16[1,512,1024]{1,0,2:T(2,128)(2,1)S(1)}) fusion(bf16[2,512,1024]{1,0,2:T(2,128)(2,1)S(1)} %broadcast_select_fusion.1), kind=kLoop, calls=%fused_computation.58 | loop fusion | bytes 4194304 | tf_op jit(solution)/shard_map/slice | solution.py:16
  97.1 2.6 %copy.10 = bf16[1,512,1024]{2,1,0:T(8,128)(2,1)S(1)} copy(bf16[1,512,1024]{1,0,2:T(2,128)(2,1)S(1)} %get-tuple-element.5) | data formatting | bytes 2097152 | tf_op jit(solution)/shard_map/slice | solution.py:15
  99.7 0.0 copy-start.1
  99.8 2.4 %copy.9 = bf16[1,2,256,512]{3,2,1,0:T(8,128)(2,1)S(1)} copy(bf16[1,2,256,512]{2,0,3,1:T(2,128)(2,1)} %get-tuple-element.8) | data formatting | bytes 1048576 | tf_op jit(solution)/shard_map/slice | solution.py:15
  102.2 4.6 %copy.12 = bf16[1,512,1024]{2,1,0:T(8,128)(2,1)S(1)} copy(bf16[1,512,1024]{1,0,2:T(2,128)(2,1)} %get-tuple-element.4) | data formatting | bytes 2097152 | tf_op jit(solution)/shard_map/slice | solution.py:16
  106.7 0.0 copy-done.1
  106.8 0.7 fusion.16
  107.5 0.7 fusion.14
  108.2 0.7 convolution_add_fusion
  108.9 0.7 convolution_subtract_fusion
  109.6 2.5 %pad_maximum_fusion = f32[512,2048]{1,0:T(8,128)} fusion(f32[512,1024]{1,0:T(8,128)S(1)} %convolution_add_fusion, f32[512,1024]{1,0:T(8,128)S(1)} %convolution_subtract_fusion), kind=kLoop, calls=%fused_computation.1 | loop fusion | flops 1048576 | bytes 8388608 | tf_op jit(solution)/shard_map/concatenate | solution.py:48
  112.1 0.0 reduce-scatter.2.cloned.1.call-update
  112.1 0.2 all-gather.2.cloned.1.call-start
  112.3 14.5 %reduce-scatter.2.cloned.1.call-done = f32[256,2048]{1,0:T(8,128)} async-done(((f32[512,2048]{1,0:T(8,128)}), f32[256,2048]{1,0:T(8,128)}) %reduce-scatter.2.cloned.1.call-update) | async-done | bytes 2097168 | tf_op jit(solution)/shard_map/reduce_scatter | solution.py:47
  126.9 1.7 convert.20
  128.6 0.1 slice_bitcast_fusion.15
  128.7 0.1 pad_maximum_fusion.2
  128.8 1.9 collective-permute-start.1
  130.7 0.0 copy-done
  130.7 0.6 constant_dynamic-slice_fusion
  131.9 22.3 %collective-permute-done.1 = bf16[2,256,1024]{2,1,0:T(8,128)(2,1)S(1)} collective-permute-done((bf16[2,256,1024]{2,1,0:T(8,128)(2,1)S(1)}, bf16[2,256,1024]{2,1,0:T(8,128)(2,1)S(1)}, u32[]{:S(2)}, u32[]{:S(2)}) %collective-permute-start.1) | collective-permute-done | bytes 1048608 | tf_op jit(solution)/shard_map/ppermute | solution.py:10
  154.2 0.1 broadcast_select_fusion.5
  154.4 1.8 collective-permute-start.2
  156.1 23.0 %collective-permute-done.2 = bf16[2,256,1024]{2,1,0:T(8,128)(2,1)} collective-permute-done((bf16[2,256,1024]{2,1,0:T(8,128)(2,1)S(1)}, bf16[2,256,1024]{2,1,0:T(8,128)(2,1)}, u32[]{:S(2)}, u32[]{:S(2)}) %collective-permute-start.2) | collective-permute-done | bytes 1048608 | tf_op jit(solution)/shard_map/ppermute | solution.py:10
  179.1 1.5 broadcast_select_fusion.4
  180.6 1.5 pad_maximum_fusion.1
  182.1 0.0 all-gather.2.cloned.1.call-update
  182.1 0.7 copy-done.3
  182.8 1.5 collective-permute-start.3
  184.3 2.1 %collective-permute-done.3 = f32[2,1024]{1,0:T(2,128)S(1)} collective-permute-done((f32[2,1024]{1,0:T(2,128)S(1)}, f32[2,1024]{1,0:T(2,128)S(1)}, u32[]{:S(2)}, u32[]{:S(2)}) %collective-permute-start.3) | collective-permute-done | bytes 8224 | tf_op jit(solution)/shard_map/ppermute | solution.py:10
  186.5 1.5 collective-permute-start.4
  188.0 2.1 %collective-permute-done.4 = f32[2,1024]{1,0:T(2,128)S(1)} collective-permute-done((f32[2,1024]{1,0:T(2,128)S(1)}, f32[2,1024]{1,0:T(2,128)S(1)}, u32[]{:S(2)}, u32[]{:S(2)}) %collective-permute-start.4) | collective-permute-done | bytes 8224 | tf_op jit(solution)/shard_map/ppermute | solution.py:10
  190.1 0.2 fusion.20
  190.3 6.5 %all-gather.2.cloned.1.call-done = bf16[2,1024,1024]{2,1,0:T(8,128)(2,1)} async-done(((bf16[2,512,1024]{2,1,0:T(8,128)(2,1)}), bf16[2,1024,1024]{2,1,0:T(8,128)(2,1)}) %all-gather.2.cloned.1.call-update) | async-done | bytes 4194320 | tf_op jit(solution)/shard_map/all_gather | solution.py:62
  196.9 2.2 %fusion.1 = f32[128,1024]{1,0:T(8,128)S(1)} fusion(bf16[2,1024,1024]{2,1,0:T(8,128)(2,1)} %all-gather.2.cloned.1.call-done, bf16[2,128,1024]{2,1,0:T(8,128)(2,1)S(1)} %fusion.20), kind=kOutput, calls=%fused_computation.9 | convolution fusion | flops 268435456 | bytes 2883584 | tf_op jit(solution)/shard_map/dot_general | solution.py:19
  199.1 2.1 fusion.8
  201.2 0.3 convolution_bitcast_fusion
  201.5 0.3 convolution_bitcast_fusion.2
  201.8 0.0 copy-done.5
  201.8 0.5 fusion.4
  202.3 0.5 fusion.7
  202.7 0.2 fusion.10
  203.0 0.4 fusion.12
  203.4 0.9 pad_maximum_fusion.4
  204.2 0.6 maximum_bitcast_fusion
  (7 shorter events, 0.0 us)
Async XLA Ops:
  7.2 123.5 %copy-start = (s32[4,1]{0,1:T(1,128)S(1)}, s32[4,1]{0,1:T(1,128)}, u32[]{:S(2)}) copy-start(s32[4,1]{0,1:T(1,128)} %param.8) | copy-start | bytes 52
  7.2 6.2 %copy-start.2 = (s32[1,1,1024]{2,1,0:T(1,128)S(1)}, s32[1,1,1024]{2,1,0:T(1,128)}, u32[]{:S(2)}) copy-start(s32[1,1,1024]{2,1,0:T(1,128)} %param.6) | copy-start | bytes 12292
  7.2 119.7 %reduce-scatter.2.cloned.1.call-start = ((), (), s32[]{:S(2)}) async-start(), calls=%async_computation.2 | async-start | bytes 6291456 | tf_op jit(solution)/shard_map/reduce_scatter | solution.py:47
  20.9 7.6 %copy-start.4 = (s32[4,2]{0,1:T(2,128)S(1)}, s32[4,2]{0,1:T(2,128)}, u32[]{:S(2)}) copy-start(s32[4,2]{0,1:T(2,128)} %param.7) | copy-start | bytes 100
  25.5 48.9 %collective-permute-start = (bf16[2,512,1024]{1,0,2:T(2,128)(2,1)}, bf16[2,512,1024]{1,0,2:T(2,128)(2,1)}, u32[]{:S(2)}, u32[]{:S(2)}) collective-permute-start(bf16[2,512,1024]{1,0,2:T(2,128)(2,1)} %fusion), channel_id=1, source_target_pairs={{0,4},{4,0},{8,12},{12,8},{16,20},{20,16},{24,28},{28,24},{1,5},{5... | collective-permute-start | bytes 6291464 | tf_op jit(solution)/shard_map/ppermute | solution.py:10
  99.7 7.0 %copy-start.1 = (bf16[1,2,256,512]{3,2,1,0:T(8,128)(2,1)S(1)}, bf16[1,2,256,512]{3,2,1,0:T(8,128)(2,1)}, u32[]{:S(2)}) copy-start(bf16[1,2,256,512]{3,2,1,0:T(8,128)(2,1)} %copy.11) | copy-start | bytes 1572868
  112.1 84.8 %all-gather.2.cloned.1.call-start = ((), (), s32[]{:S(2)}) async-start(), calls=%async_computation.3 | async-start | bytes 6291456 | tf_op jit(solution)/shard_map/all_gather | solution.py:62
  128.8 25.5 %collective-permute-start.1 = (bf16[2,256,1024]{2,1,0:T(8,128)(2,1)S(1)}, bf16[2,256,1024]{2,1,0:T(8,128)(2,1)S(1)}, u32[]{:S(2)}, u32[]{:S(2)}) collective-permute-start(bf16[2,256,1024]{2,1,0:T(8,128)(2,1)S(1)} %pad_maximum_fusion.2), channel_id=1, source_target_pairs={{0,2},{2,0},{1,3},{3,1},{4,6},{6,4},{5,7},{7,5},{8,10},{10,8},{9,1... | collective-permute-start | bytes 3145736 | tf_op jit(solution)/shard_map/ppermute | solution.py:10
  154.4 24.7 %collective-permute-start.2 = (bf16[2,256,1024]{2,1,0:T(8,128)(2,1)S(1)}, bf16[2,256,1024]{2,1,0:T(8,128)(2,1)}, u32[]{:S(2)}, u32[]{:S(2)}) collective-permute-start(bf16[2,256,1024]{2,1,0:T(8,128)(2,1)S(1)} %broadcast_select_fusion.5), channel_id=1, source_target_pairs={{0,4},{4,0},{8,12},{12,8},{16,20},{20,16},{24,28},{28,24},{1,5},{5... | collective-permute-start | bytes 3145736 | tf_op jit(solution)/shard_map/ppermute | solution.py:10
  182.1 0.7 copy-start.3
  182.8 3.7 %collective-permute-start.3 = (f32[2,1024]{1,0:T(2,128)S(1)}, f32[2,1024]{1,0:T(2,128)S(1)}, u32[]{:S(2)}, u32[]{:S(2)}) collective-permute-start(f32[2,1024]{1,0:T(2,128)S(1)} %bitcast.112), channel_id=1, source_target_pairs={{0,4},{4,0},{8,12},{12,8},{16,20},{20,16},{24,28},{28,24},{1,5},{5... | collective-permute-start | bytes 24584 | tf_op jit(solution)/shard_map/ppermute | solution.py:10
  186.5 3.7 %collective-permute-start.4 = (f32[2,1024]{1,0:T(2,128)S(1)}, f32[2,1024]{1,0:T(2,128)S(1)}, u32[]{:S(2)}, u32[]{:S(2)}) collective-permute-start(f32[2,1024]{1,0:T(2,128)S(1)} %bitcast_add_fusion), channel_id=1, source_target_pairs={{0,2},{2,0},{1,3},{3,1},{4,6},{6,4},{5,7},{7,5},{8,10},{10,8},{9,1... | collective-permute-start | bytes 24584 | tf_op jit(solution)/shard_map/ppermute | solution.py:10
  196.9 4.9 %copy-start.5 = (bf16[2,1024,1024]{2,1,0:T(8,128)(2,1)S(1)}, bf16[2,1024,1024]{2,1,0:T(8,128)(2,1)}, u32[]{:S(2)}) copy-start(bf16[2,1024,1024]{2,1,0:T(8,128)(2,1)} %all-gather.2.cloned.1.call-done) | copy-start | bytes 12582916
Sparse Core Ops, SparseCore 0:
  112.2 14.5 reduce-scatter.1
  182.3 14.5 all-gather.1
